TPU v7x, 32 devices: a whole 2x2x4 slice. The times are simulated.
32 devices in a mesh: group: 2 (over y), tm: 4 (over z), seq: 2 (over x), mp: 2 (over core).
Axes of the slice: x: 2, y: 2, z: 4, core: 2. Of those that a mesh axis runs over, the one named last changes fastest.
Arguments:
- states: bfloat16 [8, 128, 5120], P(('group', 'tm'), 'seq'), parts along dimension 0, may hold values from -6 to 6
- start_step: int32 [2], P('group'), parts along dimension 0, may hold values from 0 to 96
- w_qkv: bfloat16 [3, 5120, 3072], P(None, 'tm', ('seq', 'mp')), may hold values from -0.078125 to 0.078125
- qk_gain: float32 [2, 3072], P(None, ('seq', 'mp')), may hold values from 0.25 to 1.75
- w_out: bfloat16 [5120, 3072], P('tm', ('seq', 'mp')), may hold values from -0.109375 to 0.109375
- time_proj: bfloat16 [256, 15360], P('tm'), may hold values from -0.375 to 0.375
Outputs:
- displacement: float32 [8, 128, 5120], P(('group', 'tm'), 'seq', 'mp'), parts along dimension 0
There are 2 independent parts, one for each index of `group`. A program takes and returns all parts, laid end to end along the dimension named above; an argument that names none is the same for every part. Nothing has to cross between parts.
Inputs may be any that keep to these rules, and one draw needn't show every extreme that they name: `start_step`: the window lies inside the trajectory.
All inputs are finite; a program needn't handle non-finite values.
Results may differ from a plain program's by a relative error of at most 0.0029.
Values may be sent and summed in bfloat16 or wider, within the bound.
No kernel may reach another device: no remote copies, remote signals or barrier semaphores. Data moves between devices by JAX's collectives and lax.ppermute only.
A program may use at most 128 MiB of HBM per device.

v0:
```python
import jax
import jax.numpy as jnp
from jax import lax
from jax.sharding import PartitionSpec as P

HEAD_DIM = 128
FREQ = 256
STEPS = 100
sample_shift = 5.0
norm_eps = 1e-06


def from_behind(block, axis, distance):
    devices = range(lax.axis_size(axis))
    route = [(i - distance, i) for i in devices if i - distance in devices]
    return lax.ppermute(block, axis, route)


def sigma_of(index):
    unit = 1.0 - index.astype(jnp.float32) / jnp.float32(STEPS)
    return sample_shift * unit / (1.0 + (sample_shift - 1.0) * unit)


def embed_time(sigma_now):
    half_freq = FREQ // 2
    ranks = jnp.arange(half_freq).astype(jnp.float32)
    freqs = jnp.exp(-jnp.log(jnp.float32(10000.0)) * ranks / jnp.float32(half_freq))
    angles = (1000.0 * sigma_now)[:, None] * freqs[None, :]
    return jnp.concatenate([jnp.cos(angles), jnp.sin(angles)], axis=1).astype(jnp.bfloat16)


def head_norm(values, gain, frames, seq_len, heads_dev):
    shaped = values.reshape(frames, seq_len, heads_dev, HEAD_DIM)
    meansq = jnp.mean(shaped * shaped, axis=-1, keepdims=True)
    scaled = shaped * lax.rsqrt(meansq + norm_eps) * gain.reshape(heads_dev, HEAD_DIM)
    return scaled.astype(jnp.bfloat16)


def attend(query, keys, values):
    frames, seq_len, heads_dev, head_size = query.shape
    block = min(seq_len, 512)
    blocks = seq_len // block
    inv_root = 1.0 / jnp.sqrt(jnp.float32(head_size))
    stacked = query.reshape(frames, blocks, block, heads_dev, head_size).transpose(1, 0, 2, 3, 4)

    def one_block(q_block):
        scores = (
            jnp.einsum("wqhd,wkhd->whqk", q_block, keys, preferred_element_type=jnp.float32)
            * inv_root
        )
        expo = jnp.exp(scores)
        probs = (expo / jnp.sum(expo, axis=-1, keepdims=True)).astype(jnp.bfloat16)
        return jnp.einsum(
            "whqk,wkhd->wqhd", probs, values, preferred_element_type=jnp.float32
        ).astype(jnp.bfloat16)

    result = lax.map(one_block, stacked)
    return result.transpose(1, 0, 2, 3, 4).reshape(frames, seq_len, heads_dev * head_size)


def on_device(states, start_step, w_qkv, qk_gain, w_out, time_proj):
    frames, tok, width = states.shape
    n_tm = lax.axis_size("tm")
    n_mp = lax.axis_size("mp")
    window = frames * n_tm
    tm_pos = lax.axis_index("tm")
    steps_idx = start_step[0] + jnp.arange(window)
    sigma_now = sigma_of(steps_idx)
    step_size = sigma_of(steps_idx + 1) - sigma_now
    emb = embed_time(sigma_now)
    freq_rows = time_proj.shape[0]
    emb_cols = lax.dynamic_slice_in_dim(emb, tm_pos * freq_rows, freq_rows, 1)
    modulation = lax.psum_scatter(
        jnp.dot(emb_cols, time_proj, preferred_element_type=jnp.float32),
        "tm",
        scatter_dimension=0,
        tiled=True,
    )
    shift = modulation[:, :width]
    scale = modulation[:, width : 2 * width]
    gate = modulation[:, 2 * width :]
    field = states.astype(jnp.float32)
    mean = jnp.mean(field, axis=-1, keepdims=True)
    centred = field - mean
    var = jnp.mean(centred * centred, axis=-1, keepdims=True)
    normed = centred * lax.rsqrt(var + norm_eps)
    hidden = (normed * (1.0 + scale[:, None, :]) + shift[:, None, :]).astype(jnp.bfloat16)
    whole = lax.all_gather(hidden, "seq", axis=1, tiled=True)
    seq_len = whole.shape[1]
    flat = whole.reshape(frames * seq_len, width)
    head_cols = w_qkv.shape[2]
    heads_dev = head_cols // HEAD_DIM
    proj = jnp.einsum(
        "rd,cdh->crh",
        flat,
        lax.all_gather(w_qkv, "tm", axis=1, tiled=True),
        preferred_element_type=jnp.float32,
    )
    query = head_norm(proj[0], qk_gain[0], frames, seq_len, heads_dev)
    keys = head_norm(proj[1], qk_gain[1], frames, seq_len, heads_dev)
    values = proj[2].astype(jnp.bfloat16).reshape(frames, seq_len, heads_dev, HEAD_DIM)
    attn = attend(query, keys, values)
    out_full = lax.all_gather(w_out, "tm", axis=0, tiled=True)
    half_width = width // n_mp
    rows = frames * tok
    first = jnp.int32(0) // rows
    pieces = []
    for offset in range(rows * lax.axis_size(("seq", "mp")) // rows):
        owner = first + offset
        segment = owner // n_mp
        column = owner % n_mp
        tokens_part = lax.dynamic_slice_in_dim(attn, segment * tok, tok, 1)
        weight_part = lax.dynamic_slice_in_dim(out_full, column * half_width, half_width, 0)
        product = jnp.einsum(
            "tsh,eh->tse", tokens_part, weight_part, preferred_element_type=jnp.float32
        )
        pieces.append(product.reshape(rows, half_width))
    out_part = lax.psum_scatter(
        jnp.concatenate(pieces, axis=0), ("seq", "mp"), scatter_dimension=0, tiled=True
    ).reshape(frames, tok, half_width)
    gate_own = lax.dynamic_slice_in_dim(gate, lax.axis_index("mp") * half_width, half_width, 1)
    own_steps = lax.dynamic_slice_in_dim(step_size, tm_pos * frames, frames, 0)
    drift = gate_own[:, None, :] * out_part
    increments = own_steps[:, None, None] * drift
    local_sums = jnp.cumsum(increments, axis=0)
    block_total = local_sums[-1]
    running = block_total
    for level in range((n_tm - 1).bit_length()):
        running = running + from_behind(running, "tm", 1 << level)
    before = running - block_total
    return before[None, :, :] + local_sums


def solution(mesh):
    return jax.shard_map(
        on_device,
        mesh=mesh,
        in_specs=(
            P(("group", "tm"), "seq", None),
            P("group"),
            P(None, "tm", ("seq", "mp")),
            P(None, ("seq", "mp")),
            P("tm", ("seq", "mp")),
            P("tm", None),
        ),
        out_specs=P(("group", "tm"), "seq", "mp"),
        check_vma=False,
    )
```

profile of v0, /device:TPU:25, one launch (start us, length us, event | category | flops | bytes accessed | tf_op | source)
XLA Modules:
  0.0 721.7 jit_solution(13477119722304982495)
XLA Ops:
  6.5 0.0 copy-start
  6.5 0.0 copy-start.6
  6.5 0.0 copy-start.2
  6.5 0.0 all-reduce.3.cloned.1.call-start
  7.4 0.5 divide_subtract_fusion
  7.9 0.1 fusion.24
  8.0 0.3 copy-done
  8.3 1.1 fusion.26
  9.4 0.0 all-reduce.3.cloned.1.call-update
  9.5 0.0 all-gather.4.cloned.1.call-start
  9.5 0.0 copy-done.2
  9.5 0.2 convert_reduce_fusion
  9.7 0.3 fusion.10
  10.1 0.0 copy-done.6
  10.1 0.6 dynamic-slice.1
  10.7 32.4 %all-reduce.3.cloned.1.call-done = f32[4,15360]{1,0:T(4,128)} async-done(((f32[4,15360]{1,0:T(4,128)}), f32[4,15360]{1,0:T(4,128)}) %all-reduce.3.cloned.1.call-update) | async-done | bytes 245776
  43.0 1.7 dynamic-slice_add_fusion
  44.7 1.1 fusion.13
  45.8 0.0 all-gather.4.cloned.1.call-update
  45.9 0.0 copy-start.4
  45.9 0.0 all-gather.6.cloned.1.call-start
  45.9 0.7 all-gather.6.cloned.1.call-update
  46.6 0.0 all-gather.8.cloned.1.call-start
  46.7 0.5 all-gather.8.cloned.1.call-update
  47.2 0.0 reduce-scatter.2.cloned.1.call-start
  47.2 0.0 copy-done.4
  47.3 25.9 %all-gather.4.cloned.1.call-done = bf16[1,128,5120]{2,1,0:T(8,128)(2,1)} async-done(((bf16[1,64,5120]{2,1,0:T(8,128)(2,1)}), bf16[1,128,5120]{2,1,0:T(8,128)(2,1)}) %all-gather.4.cloned.1.call-update) | async-done | bytes 1310736 | tf_op jit(solution)/shard_map/all_gather | solution.py:88
  73.2 398.3 %all-gather.6.cloned.1.call-done = bf16[3,5120,768]{2,1,0:T(8,128)(2,1)} async-done(((bf16[3,1280,768]{2,1,0:T(8,128)(2,1)}), bf16[3,5120,768]{2,1,0:T(8,128)(2,1)}) %all-gather.6.cloned.1.call-update) | async-done | bytes 23592976 | tf_op jit(solution)/shard_map/all_gather | solution.py:96
  471.4 10.0 %convolution_bitcast_fusion = f32[3,128,768]{2,1,0:T(8,128)S(1)} fusion(bf16[3,5120,768]{2,1,0:T(8,128)(2,1)} %all-gather.6.cloned.1.call-done, bf16[1,128,5120]{2,1,0:T(8,128)(2,1)} %all-gather.4.cloned.1.call-done), kind=kOutput, calls=%fused_computation.13 | convolution fusion | flops 3019898880 | bytes 26083328 | tf_op jit(solution)/shard_map/rd,cdh->crh/dot_general | solution.py:93
  481.4 0.7 slice.45
  482.1 0.1 slice_multiply_fusion.1
  482.3 0.9 copy.23
  483.2 0.2 copy.21
  483.3 1.1 reduce_sum.49
  484.5 0.2 copy.22
  484.6 0.2 copy.20
  484.8 1.1 copy.19
  485.9 0.5 fusion.15
  486.4 0.2 convolution_convert_fusion
  486.7 125.4 %all-gather.8.cloned.1.call-done = bf16[5120,768]{1,0:T(8,128)(2,1)} async-done(((bf16[1280,768]{1,0:T(8,128)(2,1)}), bf16[5120,768]{1,0:T(8,128)(2,1)}) %all-gather.8.cloned.1.call-update) | async-done | bytes 7864336 | tf_op jit(solution)/shard_map/all_gather | solution.py:103
  612.1 0.0 copy-start.1
  612.1 3.6 fusion.2
  615.7 3.6 fusion.4
  619.3 0.0 copy-done.1
  619.3 1.3 fusion.6
  620.6 1.5 fusion
  622.1 1.7 pad_maximum_fusion
  623.8 0.0 copy-start.5
  623.8 0.0 reduce-scatter.2.cloned.1.call-update
  623.8 0.6 copy-done.5
  624.3 0.6 dynamic_slice.28
  624.9 1.5 dynamic-slice_reduce_fusion
  626.4 32.9 %reduce-scatter.2.cloned.1.call-done = f32[64,2560]{1,0:T(8,128)} async-done(((f32[256,2560]{1,0:T(8,128)}), f32[64,2560]{1,0:T(8,128)}) %reduce-scatter.2.cloned.1.call-update) | async-done | bytes 655376 | tf_op jit(solution)/shard_map/reduce_scatter | solution.py:118
  659.4 0.0 copy-start.3
  659.4 1.8 multiply_multiply_fusion
  661.1 1.3 collective-permute-start
  662.4 16.1 %collective-permute-done = f32[64,2560]{1,0:T(8,128)S(1)} collective-permute-done((f32[64,2560]{1,0:T(8,128)S(1)}, f32[64,2560]{1,0:T(8,128)S(1)}, u32[]{:S(2)}, u32[]{:S(2)}) %collective-permute-start) | collective-permute-done | bytes 655392 | tf_op jit(solution)/shard_map/ppermute | solution.py:16
  678.5 1.7 fusion.35
  680.2 1.3 collective-permute-start.1
  681.5 32.1 %collective-permute-done.1 = f32[64,2560]{1,0:T(8,128)S(1)} collective-permute-done((f32[64,2560]{1,0:T(8,128)S(1)}, f32[64,2560]{1,0:T(8,128)S(1)}, u32[]{:S(2)}, u32[]{:S(2)}) %collective-permute-start.1) | collective-permute-done | bytes 655392 | tf_op jit(solution)/shard_map/ppermute | solution.py:16
  713.7 0.0 copy-done.3
  713.7 1.5 fusion.16
  (7 shorter events, 0.1 us)
Async XLA Ops:
  6.5 1.8 copy-start
  6.5 3.5 copy-start.6
  6.5 3.0 copy-start.2
  6.5 36.5 %all-reduce.3.cloned.1.call-start = ((), (), s32[]{:S(2)}) async-start(), calls=%async_computation.5 | async-start | bytes 491520
  9.5 63.7 %all-gather.4.cloned.1.call-start = ((), (), s32[]{:S(2)}) async-start(), calls=%async_computation.1 | async-start | bytes 1966080 | tf_op jit(solution)/shard_map/all_gather | solution.py:88
  45.9 1.4 copy-start.4
  45.9 425.6 %all-gather.6.cloned.1.call-start = ((), (), s32[]{:S(2)}) async-start(), calls=%async_computation.2 | async-start | bytes 29491200 | tf_op jit(solution)/shard_map/all_gather | solution.py:96
  46.6 565.5 %all-gather.8.cloned.1.call-start = ((), (), s32[]{:S(2)}) async-start(), calls=%async_computation.3 | async-start | bytes 9830400 | tf_op jit(solution)/shard_map/all_gather | solution.py:103
  47.2 612.2 %reduce-scatter.2.cloned.1.call-start = ((), (), s32[]{:S(2)}) async-start(), calls=%async_computation.4 | async-start | bytes 3276800 | tf_op jit(solution)/shard_map/reduce_scatter | solution.py:118
  612.1 7.1 copy-start.1
  623.8 0.6 copy-start.5
  659.4 54.3 %copy-start.3 = (f32[64,2560]{1,0:T(8,128)S(1)}, f32[64,2560]{1,0:T(8,128)}, u32[]{:S(2)}) copy-start(f32[64,2560]{1,0:T(8,128)} %reduce-scatter.2.cloned.1.call-done) | copy-start | bytes 1966084
  661.1 17.4 %collective-permute-start = (f32[64,2560]{1,0:T(8,128)S(1)}, f32[64,2560]{1,0:T(8,128)S(1)}, u32[]{:S(2)}, u32[]{:S(2)}) collective-permute-start(f32[64,2560]{1,0:T(8,128)S(1)} %multiply_multiply_fusion), channel_id=1, source_target_pairs={{0,4},{4,8},{8,12},{1,5},{5,9},{9,13},{2,6},{6,10},{10,14},{3,7},{... | collective-permute-start | bytes 1966088 | tf_op jit(solution)/shard_map/ppermute | solution.py:16
  680.2 33.4 %collective-permute-start.1 = (f32[64,2560]{1,0:T(8,128)S(1)}, f32[64,2560]{1,0:T(8,128)S(1)}, u32[]{:S(2)}, u32[]{:S(2)}) collective-permute-start(f32[64,2560]{1,0:T(8,128)S(1)} %fusion.35), channel_id=1, source_target_pairs={{0,8},{4,12},{1,9},{5,13},{2,10},{6,14},{3,11},{7,15},{16,24},{20,... | collective-permute-start | bytes 1966088 | tf_op jit(solution)/shard_map/ppermute | solution.py:16
Sparse Core Ops, SparseCore 0:
  9.7 33.3 all-reduce.2
  46.0 27.1 all-gather.3
  74.7 396.6 all-gather.5
  472.9 139.2 all-gather.7
  623.9 35.4 reduce-scatter.1
where the time goes:
time: 722 us
  waiting for transfers between devices  664 us (92%)
  matrix products  21.8 us (3%)
  between operations  14.1 us (2%)
  other arithmetic  12 us (2%)
    all_gather x1, waiting for transfers between devices, on_device(): lax.all_gather(w_qkv, 'tm', axis=1, tiled=True)  398 us
    all_gather x1, waiting for transfers between devices, on_device(): out_full = lax.all_gather(w_out, 'tm', axis=0, tiled=True)  125 us
    ppermute x2, waiting for transfers between devices, from_behind(): return lax.ppermute(block, axis, route)  48.2 us
    unnamed x6, waiting for transfers between devices  33.6 us
    reduce_scatter x1, waiting for transfers between devices, on_device(): lax.psum_scatter(jnp.concatenate(pieces, axis=0), ('seq', 'mp'), scatter_...  32.9 us
    all_gather x1, waiting for transfers between devices, on_device(): whole = lax.all_gather(hidden, 'seq', axis=1, tiled=True)  25.9 us
  transfers between devices with their start and end apart: 7, of which 7 were waited for; matrix products, arithmetic and copies ran while one was open for 3% of the time, Pallas kernels for 0%

commit v1 on v0

--- a/solution.py
+++ b/solution.py
@@ -8,6 +8,17 @@
 STEPS = 100
 sample_shift = 5.0
 norm_eps = 1e-06
+
+
+def around_the_ring(x, axis, dim):
+    size = lax.axis_size(axis)
+    right = [(i, (i + 1) % size) for i in range(size)]
+    parts = [x]
+    for reach in range(1, size):
+        parts = [lax.ppermute(parts[0], axis, right), *parts]
+    whole = jnp.concatenate(parts, axis=dim)
+    places = (lax.axis_index(axis) + 1) * parts[-1].shape[dim]
+    return jnp.roll(whole, places, axis=dim)
 
 
 def from_behind(block, axis, distance):
@@ -100,7 +111,7 @@
     keys = head_norm(proj[1], qk_gain[1], frames, seq_len, heads_dev)
     values = proj[2].astype(jnp.bfloat16).reshape(frames, seq_len, heads_dev, HEAD_DIM)
     attn = attend(query, keys, values)
-    out_full = lax.all_gather(w_out, "tm", axis=0, tiled=True)
+    out_full = around_the_ring(w_out, "tm", 0)
     half_width = width // n_mp
     rows = frames * tok
     first = jnp.int32(0) // rows

time: 722 us -> 683 us (0.946)
  waiting for transfers between devices: 664 us -> 598 us
  local copies, waits for them, and re-layouts: 6.76 us -> 23.6 us
    ppermute x0 -> x3, waiting for transfers between devices: none -> 296 us  [around_the_ring(): parts = [lax.ppermute(parts[0], axis, right), *parts]]
    all_gather x1, waiting for transfers between devices: 398 us -> 190 us  [on_device(): lax.all_gather(w_qkv, 'tm', axis=1, tiled=True)]
    all_gather x1 -> x0, waiting for transfers between devices: 125 us -> none  [on_device(): out_full = lax.all_gather(w_out, 'tm', axis=0, tiled=True)]
    all_gather x1, waiting for transfers between devices: 25.9 us -> 0.01 us  [on_device(): whole = lax.all_gather(hidden, 'seq', axis=1, tiled=True)]
    unnamed x15 -> x22, local copies, waits for them, and re-layouts: 1.47 us -> 19.3 us
    unnamed x6 -> x5, waiting for transfers between devices: 33.6 us -> 30.5 us
  transfers between devices with their start and end apart: 7 -> 9, of which waited for: 7 -> 8; matrix products, arithmetic and copies ran while one was open for 3% -> 3% of each run, Pallas kernels for 0% -> 0%
where the time goes in v1:
time: 683 us
  waiting for transfers between devices  598 us (88%)
  matrix products  25.9 us (4%)
  local copies, waits for them, and re-layouts  23.6 us (3%)
  between operations  14.2 us (2%)
  other arithmetic  13.6 us (2%)
  starting transfers between devices  7.43 us (1%)
    ppermute x3, waiting for transfers between devices, around_the_ring(): parts = [lax.ppermute(parts[0], axis, right), *parts]  296 us
    all_gather x1, waiting for transfers between devices, on_device(): lax.all_gather(w_qkv, 'tm', axis=1, tiled=True)  190 us
    ppermute x2, waiting for transfers between devices, from_behind(): return lax.ppermute(block, axis, route)  48.2 us
    reduce_scatter x1, waiting for transfers between devices, on_device(): lax.psum_scatter(jnp.concatenate(pieces, axis=0), ('seq', 'mp'), scatter_...  33.1 us
    unnamed x5, waiting for transfers between devices  30.5 us
    unnamed x22, local copies, waits for them, and re-layouts  19.3 us
    dot_general x4, matrix products, on_device(): jnp.einsum('tsh,eh->tse', tokens_part, weight_part, preferred_element_typ...  14.1 us
  transfers between devices with their start and end apart: 9, of which 8 were waited for; matrix products, arithmetic and copies ran while one was open for 3% of the time, Pallas kernels for 0%

profile of v1, /device:TPU:25, one launch (start us, length us, event | category | flops | bytes accessed | tf_op | source)
XLA Modules:
  0.0 682.6 jit_solution(15492071189464584113)
XLA Ops:
  6.5 0.0 copy-start
  6.5 0.0 all-reduce.3.cloned.1.call-start
  7.4 0.1 fusion.24
  7.5 0.6 copy-done
  8.1 1.1 fusion.26
  9.2 0.0 all-reduce.3.cloned.1.call-update
  9.3 0.0 all-gather.3.cloned.1.call-start
  9.3 1.3 convert_reduce_fusion
  10.6 1.4 fusion.10
  12.0 1.3 dynamic-slice.1
  13.3 29.7 %all-reduce.3.cloned.1.call-done = f32[4,15360]{1,0:T(4,128)} async-done(((f32[4,15360]{1,0:T(4,128)}), f32[4,15360]{1,0:T(4,128)}) %all-reduce.3.cloned.1.call-update) | async-done | bytes 245776
  43.0 1.7 dynamic-slice_add_fusion
  44.7 0.0 copy-done.5
  44.7 0.0 copy-start.2
  44.7 0.0 copy-start.6
  44.7 1.1 fusion.13
  45.9 0.0 all-gather.3.cloned.1.call-update
  45.9 0.0 all-gather.5.cloned.1.call-start
  45.9 0.7 all-gather.5.cloned.1.call-update
  46.6 0.0 reduce-scatter.2.cloned.1.call-start
  46.7 0.0 copy-done.2
  46.7 1.4 collective-permute-start
  48.0 40.3 %collective-permute-done = bf16[1280,768]{1,0:T(8,128)(2,1)S(1)} collective-permute-done((bf16[1280,768]{1,0:T(8,128)(2,1)S(1)}, bf16[1280,768]{1,0:T(8,128)(2,1)S(1)}, u32[]{:S(2)}, u32[]{:S(2)}) %collective-permute-start) | collective-permute-done | bytes 1966112 | tf_op jit(solution)/shard_map/ppermute | solution.py:18
  88.3 1.3 copy-done.3
  89.6 3.4 collective-permute-start.1
  93.0 118.6 %collective-permute-done.1 = bf16[1280,768]{1,0:T(8,128)(2,1)} collective-permute-done((bf16[1280,768]{1,0:T(8,128)(2,1)S(1)}, bf16[1280,768]{1,0:T(8,128)(2,1)}, u32[]{:S(2)}, u32[]{:S(2)}) %collective-permute-start.1) | collective-permute-done | bytes 1966112 | tf_op jit(solution)/shard_map/ppermute | solution.py:18
  211.6 0.0 collective-permute-start.2
  211.6 0.0 copy-done.6
  211.6 137.3 %collective-permute-done.2 = bf16[1280,768]{1,0:T(8,128)(2,1)} collective-permute-done((bf16[1280,768]{1,0:T(8,128)(2,1)}, bf16[1280,768]{1,0:T(8,128)(2,1)}, u32[]{:S(2)}, u32[]{:S(2)}) %collective-permute-start.2) | collective-permute-done | bytes 1966112 | tf_op jit(solution)/shard_map/ppermute | solution.py:18
  349.0 3.0 constant_dynamic-update-slice_fusion.7
  352.0 3.0 constant_dynamic-update-slice_fusion.6
  355.0 0.0 copy-done.4
  355.0 1.4 constant_dynamic-update-slice_fusion.5
  356.4 1.4 constant_dynamic-update-slice_fusion.4
  357.8 3.0 constant_dynamic-update-slice_fusion.3
  360.8 2.9 constant_dynamic-update-slice_fusion.2
  363.7 1.4 constant_dynamic-update-slice_fusion.1
  365.1 1.4 constant_dynamic-update-slice_fusion
  366.5 189.9 %all-gather.5.cloned.1.call-done = bf16[3,5120,768]{2,1,0:T(8,128)(2,1)} async-done(((bf16[3,1280,768]{2,1,0:T(8,128)(2,1)}), bf16[3,5120,768]{2,1,0:T(8,128)(2,1)}) %all-gather.5.cloned.1.call-update) | async-done | bytes 23592976 | tf_op jit(solution)/shard_map/all_gather | solution.py:107
  556.4 10.0 %convolution_bitcast_fusion = f32[3,128,768]{2,1,0:T(8,128)S(1)} fusion(bf16[3,5120,768]{2,1,0:T(8,128)(2,1)} %all-gather.5.cloned.1.call-done, bf16[1,128,5120]{2,1,0:T(8,128)(2,1)} %all-gather.3.cloned.1.call-done), kind=kOutput, calls=%fused_computation.13 | convolution fusion | flops 3019898880 | bytes 26083328 | tf_op jit(solution)/shard_map/rd,cdh->crh/dot_general | solution.py:104
  566.4 0.1 slice_multiply_fusion.1
  566.5 0.2 copy.19
  566.7 0.2 copy.21
  566.9 0.2 copy.23
  567.1 0.2 copy.22
  567.3 0.2 copy.20
  567.4 0.5 fusion.15
  568.0 0.2 convolution_convert_fusion
  568.2 3.6 fusion.4
  571.8 3.4 fusion.6
  575.2 3.6 fusion
  578.8 3.4 fusion.2
  582.3 1.7 pad_maximum_fusion
  583.9 0.0 reduce-scatter.2.cloned.1.call-update
  584.0 0.6 dynamic_slice.36
  584.6 1.5 dynamic-slice_reduce_fusion
  586.1 33.1 %reduce-scatter.2.cloned.1.call-done = f32[64,2560]{1,0:T(8,128)} async-done(((f32[256,2560]{1,0:T(8,128)}), f32[64,2560]{1,0:T(8,128)}) %reduce-scatter.2.cloned.1.call-update) | async-done | bytes 655376 | tf_op jit(solution)/shard_map/reduce_scatter | solution.py:129
  619.2 1.7 multiply_multiply_fusion
  620.9 1.3 collective-permute-start.3
  622.2 16.0 %collective-permute-done.3 = f32[64,2560]{1,0:T(8,128)S(1)} collective-permute-done((f32[64,2560]{1,0:T(8,128)S(1)}, f32[64,2560]{1,0:T(8,128)S(1)}, u32[]{:S(2)}, u32[]{:S(2)}) %collective-permute-start.3) | collective-permute-done | bytes 655392 | tf_op jit(solution)/shard_map/ppermute | solution.py:27
  638.2 1.7 fusion.39
  640.0 1.3 collective-permute-start.4
  641.3 32.2 %collective-permute-done.4 = f32[64,2560]{1,0:T(8,128)S(1)} collective-permute-done((f32[64,2560]{1,0:T(8,128)S(1)}, f32[64,2560]{1,0:T(8,128)S(1)}, u32[]{:S(2)}, u32[]{:S(2)}) %collective-permute-start.4) | collective-permute-done | bytes 655392 | tf_op jit(solution)/shard_map/ppermute | solution.py:27
  673.4 2.6 fusion.16
  (16 shorter events, 0.2 us)
Async XLA Ops:
  6.5 1.6 copy-start
  6.5 38.2 %copy-start.5 = (bf16[1,64,5120]{2,1,0:T(8,128)(2,1)S(1)}, bf16[1,64,5120]{2,1,0:T(8,128)(2,1)}, u32[]{:S(2)}) copy-start(bf16[1,64,5120]{2,1,0:T(8,128)(2,1)} %param.6) | copy-start | bytes 1966084
  6.5 36.5 %all-reduce.3.cloned.1.call-start = ((), (), s32[]{:S(2)}) async-start(), calls=%async_computation.4 | async-start | bytes 491520
  9.3 357.3 %all-gather.3.cloned.1.call-start = ((), (), s32[]{:S(2)}) async-start(), calls=%async_computation.1 | async-start | bytes 1966080 | tf_op jit(solution)/shard_map/all_gather | solution.py:99
  44.7 2.0 copy-start.2
  44.7 166.9 %copy-start.6 = (f32[2,768]{1,0:T(2,128)S(1)}, f32[2,768]{1,0:T(2,128)}, u32[]{:S(2)}) copy-start(f32[2,768]{1,0:T(2,128)} %param.9) | copy-start | bytes 18436
  45.9 510.5 %all-gather.5.cloned.1.call-start = ((), (), s32[]{:S(2)}) async-start(), calls=%async_computation.2 | async-start | bytes 29491200 | tf_op jit(solution)/shard_map/all_gather | solution.py:107
  46.6 572.5 %reduce-scatter.2.cloned.1.call-start = ((), (), s32[]{:S(2)}) async-start(), calls=%async_computation.3 | async-start | bytes 3276800 | tf_op jit(solution)/shard_map/reduce_scatter | solution.py:129
  46.7 41.6 %collective-permute-start = (bf16[1280,768]{1,0:T(8,128)(2,1)S(1)}, bf16[1280,768]{1,0:T(8,128)(2,1)S(1)}, u32[]{:S(2)}, u32[]{:S(2)}) collective-permute-start(bf16[1280,768]{1,0:T(8,128)(2,1)S(1)} %copy-done.2), channel_id=1, source_target_pairs={{0,4},{4,8},{8,12},{12,0},{1,5},{5,9},{9,13},{13,1},{2,6},{6,10},{... | collective-permute-start | bytes 5898248 | tf_op jit(solution)/shard_map/ppermute | solution.py:18
  88.3 1.3 copy-start.3
  89.6 122.0 %collective-permute-start.1 = (bf16[1280,768]{1,0:T(8,128)(2,1)S(1)}, bf16[1280,768]{1,0:T(8,128)(2,1)}, u32[]{:S(2)}, u32[]{:S(2)}) collective-permute-start(bf16[1280,768]{1,0:T(8,128)(2,1)S(1)} %collective-permute-done), channel_id=1, source_target_pairs={{0,4},{4,8},{8,12},{12,0},{1,5},{5,9},{9,13},{13,1},{2,6},{6,10},{... | collective-permute-start | bytes 5898248 | tf_op jit(solution)/shard_map/ppermute | solution.py:18
  211.6 137.4 %collective-permute-start.2 = (bf16[1280,768]{1,0:T(8,128)(2,1)}, bf16[1280,768]{1,0:T(8,128)(2,1)}, u32[]{:S(2)}, u32[]{:S(2)}) collective-permute-start(bf16[1280,768]{1,0:T(8,128)(2,1)} %collective-permute-done.1), channel_id=1, source_target_pairs={{0,4},{4,8},{8,12},{12,0},{1,5},{5,9},{9,13},{13,1},{2,6},{6,10},{... | collective-permute-start | bytes 5898248 | tf_op jit(solution)/shard_map/ppermute | solution.py:18
  211.6 143.4 %copy-start.4 = (bf16[1280,768]{1,0:T(8,128)(2,1)S(1)}, bf16[1280,768]{1,0:T(8,128)(2,1)}, u32[]{:S(2)}) copy-start(bf16[1280,768]{1,0:T(8,128)(2,1)} %copy-done.3) | copy-start | bytes 5898244
  583.9 92.1 %copy-start.1 = (bf16[64,15360]{1,0:T(8,128)(2,1)S(1)}, bf16[64,15360]{1,0:T(8,128)(2,1)}, u32[]{:S(2)}) copy-start(bf16[64,15360]{1,0:T(8,128)(2,1)} %param.11) | copy-start | bytes 5898244
  620.9 17.3 %collective-permute-start.3 = (f32[64,2560]{1,0:T(8,128)S(1)}, f32[64,2560]{1,0:T(8,128)S(1)}, u32[]{:S(2)}, u32[]{:S(2)}) collective-permute-start(f32[64,2560]{1,0:T(8,128)S(1)} %multiply_multiply_fusion), channel_id=1, source_target_pairs={{0,4},{4,8},{8,12},{1,5},{5,9},{9,13},{2,6},{6,10},{10,14},{3,7},{... | collective-permute-start | bytes 1966088 | tf_op jit(solution)/shard_map/ppermute | solution.py:27
  640.0 33.5 %collective-permute-start.4 = (f32[64,2560]{1,0:T(8,128)S(1)}, f32[64,2560]{1,0:T(8,128)S(1)}, u32[]{:S(2)}, u32[]{:S(2)}) collective-permute-start(f32[64,2560]{1,0:T(8,128)S(1)} %fusion.39), channel_id=1, source_target_pairs={{0,8},{4,12},{1,9},{5,13},{2,10},{6,14},{3,11},{7,15},{16,24},{20,... | collective-permute-start | bytes 1966088 | tf_op jit(solution)/shard_map/ppermute | solution.py:27
Sparse Core Ops, SparseCore 0:
  9.7 33.3 all-reduce.2
  46.0 27.1 all-gather.2
  74.8 481.5 all-gather.4
  584.1 35.0 reduce-scatter.1
